TPU v7x, 512 devices: a whole 4x4x16 slice. The times are simulated.
512 devices in a mesh: tok: 32 (over z, core), feat: 16 (over y, x).
Axes of the slice: x: 4, y: 4, z: 16, core: 2. Of those that a mesh axis runs over, the one named last changes fastest.
Arguments:
- tokens: bfloat16 [12288, 1408], P(('tok', 'feat')), may hold values from -24 to 24
- segment_ids: int32 [12288], P('tok'), may hold values from 0 to 1023, as said below
- owners: int32 [1024], P('tok'), may hold values from 0 to 31, as said below
- project_in: bfloat16 [1408, 3, 1408], P(None, None, 'feat'), may hold values from -2 to 2
- project_out: bfloat16 [1408, 1408], P('feat'), may hold values from -0.15625 to 0.15625
- weight_up: bfloat16 [1408, 6144], P('tok', 'feat'), may hold values from -0.15625 to 0.15625
- weight_down: bfloat16 [6144, 1408], P('feat', 'tok'), may hold values from -0.078125 to 0.078125
- weight_merge: bfloat16 [5632, 4096], P(None, 'feat'), may hold values from -0.078125 to 0.078125
- gain_attend: bfloat16 [1408], replicated, may hold values from 0.25 to 1.75
- gain_hidden: bfloat16 [1408], replicated, may hold values from 0.25 to 1.75
- gain_final: bfloat16 [1408], replicated, may hold values from 0.25 to 1.75
Outputs:
- routed: bfloat16 [16384, 4096], P('tok', 'feat')
Inputs may be any that keep to these rules, and one draw needn't show every extreme that they name: `segment_ids`: patches 384 * s to 384 * s + 383 form shard s; their ids never fall, run without gaps and lie in 32 * s to 32 * s + 31; in every shard but the last they start at 32 * s, in the last they end at 1023. Every segment has 16 to 64 patches, a multiple of 4, and every shard holds one of 64 patches. Each 2x2 window of an image is four consecutive patches. owners[g] is the tok index that owns segment g; the 32 entries from 32 * s to 32 * s + 31 are distinct.
All inputs are finite; a program needn't handle non-finite values.
Results may differ from a plain program's by a relative error of at most 0.025.
Values may be sent and summed in bfloat16 or wider, within the bound.
A program may use at most 64 MiB of HBM per device.

v0:
```python
import jax
import jax.numpy as jnp
from jax import lax
from jax.sharding import PartitionSpec as P

LEAST_UNITS = 4
MOST_UNITS = 16
HEAD_DIM = 88
epsilon = 1e-06


def layer_norm(row_block, gain_row):
    as_float = row_block.astype(jnp.float32)
    center = jnp.mean(as_float, axis=-1, keepdims=True)
    spread = jnp.mean(jnp.square(as_float - center), axis=-1, keepdims=True)
    scaled = (as_float - center) * lax.rsqrt(spread + epsilon) * gain_row.astype(jnp.float32)
    return scaled.astype(jnp.bfloat16)


def project_rows(row_block, weight_block):
    return jnp.dot(
        lax.all_gather(row_block, "feat", axis=0, tiled=True),
        weight_block,
        preferred_element_type=jnp.float32,
    )


def scatter_rows(left_rows, right_rows):
    return lax.psum_scatter(
        jnp.dot(left_rows, right_rows, preferred_element_type=jnp.float32).astype(jnp.bfloat16),
        "feat",
        scatter_dimension=0,
        tiled=True,
    ).astype(jnp.float32)


def early_weights(weight_up, weight_down):
    return (weight_up, weight_down)


def upper_weight(fetched):
    return lax.all_gather(fetched[0], "tok", axis=0, tiled=True)


def lower_weight(fetched):
    return lax.all_gather(fetched[1], "tok", axis=1, tiled=True)


def attend(projected, segment_ids, head_count):
    token_count = projected.shape[0]
    parts_all = projected.reshape(token_count, 3, head_count, HEAD_DIM)
    queries = (parts_all[:, 0] * HEAD_DIM ** (-0.5)).astype(jnp.bfloat16)
    keys_here = parts_all[:, 1].astype(jnp.bfloat16)
    values_here = parts_all[:, 2].astype(jnp.bfloat16)
    scores = jnp.einsum("qhd,khd->hqk", queries, keys_here, preferred_element_type=jnp.float32)
    same_segment = segment_ids[:, None] == segment_ids[None, :]
    scores = jnp.where(same_segment[None, :, :], scores, -1e30)
    highest = jnp.max(scores, axis=-1, keepdims=True)
    raised = jnp.exp(scores - highest)
    weights_soft = (raised / jnp.sum(raised, axis=-1, keepdims=True)).astype(jnp.bfloat16)
    attended = jnp.einsum(
        "hqk,khd->qhd", weights_soft, values_here, preferred_element_type=jnp.float32
    )
    return attended.astype(jnp.bfloat16).reshape(token_count, head_count * HEAD_DIM)


def route_rows(embedded, segment_ids, owners):
    merged_count = embedded.shape[0]
    peer_count = owners.shape[0]
    least_units = max(LEAST_UNITS, (merged_count + peer_count - 1) // peer_count)
    slot_count = max(MOST_UNITS, 2 * least_units)
    first_ids = segment_ids.reshape(merged_count, 4)[:, 0]
    id_base = lax.axis_index("tok") * peer_count
    local_index = first_ids - id_base
    owner_pick = local_index[:, None] == jnp.arange(peer_count, dtype=jnp.int32)[None, :]
    owner_of = jnp.sum(jnp.where(owner_pick, owners[None, :], 0), axis=1)
    row_index = jnp.arange(merged_count, dtype=jnp.int32)
    earlier = (row_index[None, :] < row_index[:, None]) & (first_ids[None, :] == first_ids[:, None])
    within = jnp.sum(earlier.astype(jnp.int32), axis=1)
    target = owner_of * slot_count + within
    select = (
        jnp.arange(peer_count * slot_count, dtype=jnp.int32)[:, None] == target[None, :]
    ).astype(jnp.bfloat16)
    packed = jnp.dot(select, embedded, preferred_element_type=jnp.float32).astype(jnp.bfloat16)
    packed = packed.reshape(peer_count, slot_count, embedded.shape[1])
    received = lax.all_to_all(packed, "tok", split_axis=0, concat_axis=0, tiled=True)
    return received.reshape(peer_count * slot_count, embedded.shape[1])


def body(
    tokens,
    segment_ids,
    owners,
    project_in,
    project_out,
    weight_up,
    weight_down,
    weight_merge,
    gain_attend,
    gain_hidden,
    gain_final,
):
    model_width = tokens.shape[1]
    head_count = project_in.shape[2] // HEAD_DIM
    fetched = early_weights(weight_up, weight_down)
    flat_in = project_in.reshape(model_width, 3 * project_in.shape[2])
    local_count = tokens.shape[0]
    normed = layer_norm(tokens, gain_attend)
    projected = project_rows(normed, flat_in)
    attended = attend(projected, segment_ids, head_count)
    second = (tokens.astype(jnp.float32) + scatter_rows(attended, project_out)).astype(jnp.bfloat16)
    normed_hidden = layer_norm(second, gain_hidden)
    hidden = jax.nn.gelu(
        project_rows(normed_hidden, upper_weight(fetched)), approximate=False
    ).astype(jnp.bfloat16)
    residual_out = (
        second.astype(jnp.float32) + scatter_rows(hidden, lower_weight(fetched))
    ).astype(jnp.bfloat16)
    normed_final = layer_norm(residual_out, gain_final)
    merged = normed_final.reshape(local_count // 4, 4 * model_width)
    embedded = project_rows(merged, weight_merge).astype(jnp.bfloat16)
    return route_rows(embedded, segment_ids, owners)


def solution(mesh):
    return jax.shard_map(
        body,
        mesh=mesh,
        in_specs=(
            P(("tok", "feat"), None),
            P("tok"),
            P("tok"),
            P(None, None, "feat"),
            P("feat", None),
            P("tok", "feat"),
            P("feat", "tok"),
            P(None, "feat"),
            P(),
            P(),
            P(),
        ),
        out_specs=P("tok", "feat"),
        check_vma=False,
    )
```

profile of v0, /device:TPU:1, one launch (start us, length us, event | category | flops | bytes accessed | tf_op | source)
XLA Modules:
  0.0 485.8 jit_solution(15327780551669928933)
XLA Ops:
  7.4 1.2 convert_reduce_fusion.1
  8.5 1.1 fusion.58
  9.6 0.7 convert_element_type.98
  10.3 1.6 fusion.60
  12.0 62.1 %all-gather.9.cloned.1.call-done = bf16[384,1408]{1,0:T(8,128)(2,1)} async-done(((bf16[24,1408]{1,0:T(8,128)(2,1)}), bf16[384,1408]{1,0:T(8,128)(2,1)}) %all-gather.9.cloned.1.call-update) | async-done | bytes 1081360 | tf_op jit(solution)/shard_map/all_gather | solution.py:22
  74.1 2.0 fusion.104
  76.2 0.3 fusion.105
  76.5 0.4 copy-done.2
  76.9 2.6 convolution_convert_fusion.1
  79.7 0.5 all-gather.13.cloned.1.call-update
  80.2 0.5 all-gather.15.cloned.1.call-update
  80.8 86.1 %reduce-scatter.7.cloned.1.call-done = bf16[24,1408]{1,0:T(8,128)(2,1)} async-done(((bf16[384,1408]{1,0:T(8,128)(2,1)}), bf16[24,1408]{1,0:T(8,128)(2,1)}) %reduce-scatter.7.cloned.1.call-update) | async-done | bytes 67600
  167.0 1.0 convert_reduce_fusion
  168.0 0.2 fusion.55
  168.2 0.7 fusion.57
  169.0 2.2 reshape.121
  171.2 53.8 %all-gather.15.cloned.1.call-done = bf16[32,44,384]{2,1,0:T(8,128)(2,1)} async-done(((bf16[1,44,384]{2,1,0:T(8,128)(2,1)}), bf16[32,44,384]{2,1,0:T(8,128)(2,1)}) %all-gather.15.cloned.1.call-update) | async-done | bytes 1081360 | tf_op jit(solution)/shard_map/all_gather | solution.py:46
  225.1 2.2 reshape.123
  227.3 53.9 %all-gather.11.cloned.1.call-done = bf16[384,1408]{1,0:T(8,128)(2,1)} async-done(((bf16[24,1408]{1,0:T(8,128)(2,1)}), bf16[384,1408]{1,0:T(8,128)(2,1)}) %all-gather.11.cloned.1.call-update) | async-done | bytes 1081360 | tf_op jit(solution)/shard_map/all_gather | solution.py:22
  281.2 5.5 %convolution_convert_fusion = bf16[384,1408]{1,0:T(8,128)(2,1)} fusion(bf16[1408,384]{1,0:T(8,128)(2,1)} %reshape.123, bf16[384,1408]{1,0:T(8,128)(2,1)} %all-gather.11.cloned.1.call-done, bf16[1408,384]{1,0:T(8,128)(2,1)} %reshape.121), kind=kOutput, calls=%fused_computation | convolution fusion | flops 840597504 | bytes 4325376 | tf_op jit(solution)/shard_map/dot_general | solution.py:30
  286.8 0.6 copy-done.5
  287.4 87.0 %reduce-scatter.9.cloned.1.call-done = bf16[24,1408]{1,0:T(8,128)(2,1)} async-done(((bf16[384,1408]{1,0:T(8,128)(2,1)}), bf16[24,1408]{1,0:T(8,128)(2,1)}) %reduce-scatter.9.cloned.1.call-update) | async-done | bytes 67600
  374.4 1.0 convert_reduce_fusion.2
  375.5 1.1 fusion.61
  376.6 1.0 fusion.63
  377.5 0.7 reshape.124
  378.5 0.2 convert_reduce_fusion.3
  378.8 57.7 %all-gather.17.cloned.1.call-done = bf16[16,6,5632]{2,1,0:T(8,128)(2,1)} async-done(((bf16[1,6,5632]{2,1,0:T(8,128)(2,1)}), bf16[16,6,5632]{2,1,0:T(8,128)(2,1)}) %all-gather.17.cloned.1.call-update) | async-done | bytes 1081360 | tf_op jit(solution)/shard_map/all_gather | solution.py:22
  436.5 2.3 reshape.125
  438.8 2.1 convolution_convert_fusion.2
  441.0 36.8 %all_to_all.5 = bf16[32,16,256]{2,1,0:T(8,128)(2,1)S(1)} all-to-all(bf16[32,16,256]{2,1,0:T(8,128)(2,1)S(1)} %bitcast.51), channel_id=1, replica_groups=mesh['tok'=32,'feat'=16] {'tok'}, dimensions={0} | all-to-all | bytes 524288 | tf_op jit(solution)/shard_map/all_to_all | solution.py:86
  477.8 0.7 copy.13
  (38 shorter events, 0.9 us)
Async XLA Ops:
  7.4 431.5 %copy-start = (bf16[5632,256]{1,0:T(8,128)(2,1)S(1)}, bf16[5632,256]{1,0:T(8,128)(2,1)}, u32[]{:S(2)}) copy-start(bf16[5632,256]{1,0:T(8,128)(2,1)} %param.18) | copy-start | bytes 8650756
  7.4 66.7 %all-gather.9.cloned.1.call-start = ((), (), s32[]{:S(2)}) async-start(), calls=%async_computation.3 | async-start | bytes 1148928 | tf_op jit(solution)/shard_map/all_gather | solution.py:22
  11.9 64.2 %copy-start.3 = (s32[384]{0:T(512)S(1)}, s32[384]{0:T(512)}, u32[]{:S(2)}) copy-start(s32[384]{0:T(512)} %param.12) | copy-start | bytes 4612
  12.0 155.0 %reduce-scatter.7.cloned.1.call-start = ((), (), s32[]{:S(2)}) async-start(), calls=%async_computation.8 | async-start | bytes 1148928
  76.1 0.7 copy-start.2
  79.6 1.2 copy-start.4
  79.6 87.4 %copy-start.1 = (bf16[24,1408]{1,0:T(8,128)(2,1)S(1)}, bf16[24,1408]{1,0:T(8,128)(2,1)}, u32[]{:S(2)}) copy-start(bf16[24,1408]{1,0:T(8,128)(2,1)} %param.11) | copy-start | bytes 202756
  79.6 89.4 %all-gather.13.cloned.1.call-start = ((), (), s32[]{:S(2)}) async-start(), calls=%async_computation.5 | async-start | bytes 1216512 | tf_op jit(solution)/shard_map/all_gather | solution.py:42
  80.2 144.9 %all-gather.15.cloned.1.call-start = ((), (), s32[]{:S(2)}) async-start(), calls=%async_computation.6 | async-start | bytes 1216512 | tf_op jit(solution)/shard_map/all_gather | solution.py:46
  80.8 200.4 %all-gather.11.cloned.1.call-start = ((), (), s32[]{:S(2)}) async-start(), calls=%async_computation.4 | async-start | bytes 1148928 | tf_op jit(solution)/shard_map/all_gather | solution.py:22
  169.0 205.5 %reduce-scatter.9.cloned.1.call-start = ((), (), s32[]{:S(2)}) async-start(), calls=%async_computation.9 | async-start | bytes 1148928
  286.7 0.7 copy-start.5
  286.7 91.9 %copy-start.6 = (s32[32]{0:T(128)S(1)}, s32[32]{0:T(128)}, u32[]{:S(2)}) copy-start(s32[32]{0:T(128)} %param.13) | copy-start | bytes 388
  286.8 149.8 %all-gather.17.cloned.1.call-start = ((), (), s32[]{:S(2)}) async-start(), calls=%async_computation.7 | async-start | bytes 1531904 | tf_op jit(solution)/shard_map/all_gather | solution.py:22
Sparse Core Ops, SparseCore 0:
  12.1 61.9 all-gather.8
  79.7 87.1 reduce-scatter.6
  286.9 87.5 reduce-scatter.8
Sparse Core Ops, SparseCore 1:
  82.2 72.5 all-gather.12
  156.7 68.3 all-gather.14
  228.0 53.2 all-gather.10
  378.3 58.1 all-gather.16
where the time goes:
time: 486 us
  waiting for transfers between devices  402 us (83%)
  blocking collectives  36.8 us (8%)
  between operations  14.9 us (3%)
  matrix products  12.6 us (3%)
  other arithmetic  10.1 us (2%)
  local copies, waits for them, and re-layouts  9.2 us (2%)
    unnamed x9, waiting for transfers between devices  174 us
    all_gather x3, waiting for transfers between devices, project_rows(): lax.all_gather(row_block, 'feat', axis=0, tiled=True)  174 us
    all_gather x1, waiting for transfers between devices, lower_weight(): return lax.all_gather(fetched[1], 'tok', axis=1, tiled=True)  53.8 us
    all_to_all x1, blocking collectives, route_rows(): lax.all_to_all(packed, 'tok', split_axis=0, concat_axis=0, tiled=True)  36.8 us
  transfers between devices with their start and end apart: 7, of which 6 were waited for; matrix products, arithmetic and copies ran while one was open for 1% of the time, Pallas kernels for 0%

commit v1 on v0

--- a/solution.py
+++ b/solution.py
@@ -7,6 +7,19 @@
 MOST_UNITS = 16
 HEAD_DIM = 88
 epsilon = 1e-06
+
+
+def ring_gather(x, axis, dim):
+    ways = lax.axis_size(axis)
+    up = [(d, (d + 1) % ways) for d in range(ways)]
+    down = [(d, (d - 1) % ways) for d in range(ways)]
+    earlier, later = ([x], [x])
+    for _ in range(ways // 2):
+        earlier.append(lax.ppermute(earlier[-1], axis, up))
+    for _ in range((ways - 1) // 2):
+        later.append(lax.ppermute(later[-1], axis, down))
+    line = jnp.concatenate([*earlier[::-1], *later[1:]], axis=dim)
+    return jnp.roll(line, (lax.axis_index(axis) - ways // 2) * x.shape[dim], axis=dim)
 
 
 def layer_norm(row_block, gain_row):
@@ -19,9 +32,7 @@
 
 def project_rows(row_block, weight_block):
     return jnp.dot(
-        lax.all_gather(row_block, "feat", axis=0, tiled=True),
-        weight_block,
-        preferred_element_type=jnp.float32,
+        ring_gather(row_block, "feat", 0), weight_block, preferred_element_type=jnp.float32
     )
 
 

time: 486 us -> 579 us (1.19)
  waiting for transfers between devices: 402 us -> 203 us
  starting transfers between devices: 0.25 us -> 190 us
  local copies, waits for them, and re-layouts: 9.2 us -> 97.9 us
  blocking collectives: 36.8 us -> 43.9 us
    ppermute x0 -> x45, starting transfers between devices: none -> 190 us  [the longest x21 140 us: ring_gather(): later.append(lax.ppermute(later[-1], axis, down))]
    all_gather x3 -> x0, waiting for transfers between devices: 174 us -> none  [project_rows(): lax.all_gather(row_block, 'feat', axis=0, tiled=True)]
    concatenate x0 -> x3, local copies, waits for them, and re-layouts: none -> 70.9 us  [the longest x1 70.2 us: ring_gather(): jnp.roll(line, (lax.axis_index(axis) - ways // 2) * x.shape[dim], axis=dim)]
    all_gather x1, waiting for transfers between devices: 53.8 us -> 0.01 us  [lower_weight(): return lax.all_gather(fetched[1], 'tok', axis=1, tiled=True)]
    ppermute x0 -> x45, waiting for transfers between devices: none -> 18.3 us  [the longest x24 18.3 us: ring_gather(): earlier.append(lax.ppermute(earlier[-1], axis, up))]
    unnamed x19 -> x63, local copies, waits for them, and re-layouts: 9.1 us -> 26.3 us
    unnamed x9 -> x6, waiting for transfers between devices: 174 us -> 185 us
    all_to_all x1, blocking collectives: 36.8 us -> 43.9 us  [route_rows(): lax.all_to_all(packed, 'tok', split_axis=0, concat_axis=0, tiled=True)]
  transfers between devices with their start and end apart: 7 -> 49, of which waited for: 6 -> 6; matrix products, arithmetic and copies ran while one was open for 1% -> 5% of each run, Pallas kernels for 0% -> 0%
where the time goes in v1:
time: 579 us; the launch traced here: 573 us
  waiting for transfers between devices  203 us (35%)
  starting transfers between devices  190 us (33%)
  local copies, waits for them, and re-layouts  97.9 us (17%)
  blocking collectives  43.9 us (8%)
  between operations  15.9 us (3%)
  matrix products  12.1 us (2%)
  other arithmetic  10.4 us (2%)
    unnamed x6, waiting for transfers between devices  185 us
    ppermute x21, starting transfers between devices, ring_gather(): later.append(lax.ppermute(later[-1], axis, down))  140 us
    concatenate x1, local copies, waits for them, and re-layouts, ring_gather(): jnp.roll(line, (lax.axis_index(axis) - ways // 2) * x.shape[dim], axis=dim)  70.2 us
    ppermute x24, starting transfers between devices, ring_gather(): earlier.append(lax.ppermute(earlier[-1], axis, up))  49.3 us
    all_to_all x1, blocking collectives, route_rows(): lax.all_to_all(packed, 'tok', split_axis=0, concat_axis=0, tiled=True)  43.9 us
    unnamed x63, local copies, waits for them, and re-layouts  26.3 us
    ppermute x24, waiting for transfers between devices, ring_gather(): earlier.append(lax.ppermute(earlier[-1], axis, up))  18.3 us
  transfers between devices with their start and end apart: 49, of which 6 were waited for; matrix products, arithmetic and copies ran while one was open for 5% of the time, Pallas kernels for 0%

profile of v1, /device:TPU:1, one launch (start us, length us, event | category | flops | bytes accessed | tf_op | source)
XLA Modules:
  0.0 573.1 jit_solution(12973640996930477600)
XLA Ops:
  11.3 3.9 collective-permute-start
  15.3 5.4 collective-permute-done
  22.6 6.7 %collective-permute-start.8 = (bf16[24,1408]{1,0:T(8,128)(2,1)S(1)}, bf16[24,1408]{1,0:T(8,128)(2,1)S(1)}, u32[]{:S(2)}, u32[]{:S(2)}) collective-permute-start(bf16[24,1408]{1,0:T(8,128)(2,1)S(1)} %fusion.70), channel_id=1, source_target_pairs={{0,15},{1,0},{2,1},{3,2},{4,3},{5,4},{6,5},{7,6},{8,7},{9,8},{10,9... | collective-permute-start | bytes 202760 | tf_op jit(solution)/shard_map/ppermute | solution.py:20
  31.2 6.7 %collective-permute-start.9 = (bf16[24,1408]{1,0:T(8,128)(2,1)S(1)}, bf16[24,1408]{1,0:T(8,128)(2,1)S(1)}, u32[]{:S(2)}, u32[]{:S(2)}) collective-permute-start(bf16[24,1408]{1,0:T(8,128)(2,1)S(1)} %collective-permute-done.8), channel_id=1, source_target_pairs={{0,15},{1,0},{2,1},{3,2},{4,3},{5,4},{6,5},{7,6},{8,7},{9,8},{10,9... | collective-permute-start | bytes 202760 | tf_op jit(solution)/shard_map/ppermute | solution.py:20
  39.8 6.7 %collective-permute-start.10 = (bf16[24,1408]{1,0:T(8,128)(2,1)S(1)}, bf16[24,1408]{1,0:T(8,128)(2,1)S(1)}, u32[]{:S(2)}, u32[]{:S(2)}) collective-permute-start(bf16[24,1408]{1,0:T(8,128)(2,1)S(1)} %collective-permute-done.9), channel_id=1, source_target_pairs={{0,15},{1,0},{2,1},{3,2},{4,3},{5,4},{6,5},{7,6},{8,7},{9,8},{10,9... | collective-permute-start | bytes 202760 | tf_op jit(solution)/shard_map/ppermute | solution.py:20
  48.6 7.2 %collective-permute-start.11 = (bf16[24,1408]{1,0:T(8,128)(2,1)S(1)}, bf16[24,1408]{1,0:T(8,128)(2,1)S(1)}, u32[]{:S(2)}, u32[]{:S(2)}) collective-permute-start(bf16[24,1408]{1,0:T(8,128)(2,1)S(1)} %collective-permute-done.10), channel_id=1, source_target_pairs={{0,15},{1,0},{2,1},{3,2},{4,3},{5,4},{6,5},{7,6},{8,7},{9,8},{10,9... | collective-permute-start | bytes 202760 | tf_op jit(solution)/shard_map/ppermute | solution.py:20
  57.8 6.7 %collective-permute-start.12 = (bf16[24,1408]{1,0:T(8,128)(2,1)S(1)}, bf16[24,1408]{1,0:T(8,128)(2,1)}, u32[]{:S(2)}, u32[]{:S(2)}) collective-permute-start(bf16[24,1408]{1,0:T(8,128)(2,1)S(1)} %collective-permute-done.11), channel_id=1, source_target_pairs={{0,15},{1,0},{2,1},{3,2},{4,3},{5,4},{6,5},{7,6},{8,7},{9,8},{10,9... | collective-permute-start | bytes 202760 | tf_op jit(solution)/shard_map/ppermute | solution.py:20
  66.5 6.7 %collective-permute-start.13 = (bf16[24,1408]{1,0:T(8,128)(2,1)}, bf16[24,1408]{1,0:T(8,128)(2,1)}, u32[]{:S(2)}, u32[]{:S(2)}) collective-permute-start(bf16[24,1408]{1,0:T(8,128)(2,1)} %collective-permute-done.12), channel_id=1, source_target_pairs={{0,15},{1,0},{2,1},{3,2},{4,3},{5,4},{6,5},{7,6},{8,7},{9,8},{10,9... | collective-permute-start | bytes 202760 | tf_op jit(solution)/shard_map/ppermute | solution.py:20
  75.2 6.8 %collective-permute-start.14 = (bf16[24,1408]{1,0:T(8,128)(2,1)}, bf16[24,1408]{1,0:T(8,128)(2,1)S(1)}, u32[]{:S(2)}, u32[]{:S(2)}) collective-permute-start(bf16[24,1408]{1,0:T(8,128)(2,1)} %collective-permute-done.13), channel_id=1, source_target_pairs={{0,15},{1,0},{2,1},{3,2},{4,3},{5,4},{6,5},{7,6},{8,7},{9,8},{10,9... | collective-permute-start | bytes 202760 | tf_op jit(solution)/shard_map/ppermute | solution.py:20
  89.8 2.7 convolution_convert_fusion.1
  93.7 92.6 %reduce-scatter.7.cloned.1.call-done = bf16[24,1408]{1,0:T(8,128)(2,1)} async-done(((bf16[384,1408]{1,0:T(8,128)(2,1)}), bf16[24,1408]{1,0:T(8,128)(2,1)}) %reduce-scatter.7.cloned.1.call-update) | async-done | bytes 67600
  187.6 2.5 collective-permute-start.15
  190.1 5.9 %collective-permute-done.15 = bf16[24,1408]{1,0:T(8,128)(2,1)S(1)} collective-permute-done((bf16[24,1408]{1,0:T(8,128)(2,1)S(1)}, bf16[24,1408]{1,0:T(8,128)(2,1)S(1)}, u32[]{:S(2)}, u32[]{:S(2)}) %collective-permute-start.15) | collective-permute-done | bytes 67616 | tf_op jit(solution)/shard_map/ppermute | solution.py:18
  197.9 6.7 %collective-permute-start.23 = (bf16[24,1408]{1,0:T(8,128)(2,1)S(1)}, bf16[24,1408]{1,0:T(8,128)(2,1)S(1)}, u32[]{:S(2)}, u32[]{:S(2)}) collective-permute-start(bf16[24,1408]{1,0:T(8,128)(2,1)S(1)} %fusion.67), channel_id=1, source_target_pairs={{0,15},{1,0},{2,1},{3,2},{4,3},{5,4},{6,5},{7,6},{8,7},{9,8},{10,9... | collective-permute-start | bytes 202760 | tf_op jit(solution)/shard_map/ppermute | solution.py:20
  206.5 6.7 %collective-permute-start.24 = (bf16[24,1408]{1,0:T(8,128)(2,1)S(1)}, bf16[24,1408]{1,0:T(8,128)(2,1)S(1)}, u32[]{:S(2)}, u32[]{:S(2)}) collective-permute-start(bf16[24,1408]{1,0:T(8,128)(2,1)S(1)} %collective-permute-done.23), channel_id=1, source_target_pairs={{0,15},{1,0},{2,1},{3,2},{4,3},{5,4},{6,5},{7,6},{8,7},{9,8},{10,9... | collective-permute-start | bytes 202760 | tf_op jit(solution)/shard_map/ppermute | solution.py:20
  215.2 6.7 %collective-permute-start.25 = (bf16[24,1408]{1,0:T(8,128)(2,1)S(1)}, bf16[24,1408]{1,0:T(8,128)(2,1)S(1)}, u32[]{:S(2)}, u32[]{:S(2)}) collective-permute-start(bf16[24,1408]{1,0:T(8,128)(2,1)S(1)} %collective-permute-done.24), channel_id=1, source_target_pairs={{0,15},{1,0},{2,1},{3,2},{4,3},{5,4},{6,5},{7,6},{8,7},{9,8},{10,9... | collective-permute-start | bytes 202760 | tf_op jit(solution)/shard_map/ppermute | solution.py:20
  223.8 6.7 %collective-permute-start.26 = (bf16[24,1408]{1,0:T(8,128)(2,1)S(1)}, bf16[24,1408]{1,0:T(8,128)(2,1)S(1)}, u32[]{:S(2)}, u32[]{:S(2)}) collective-permute-start(bf16[24,1408]{1,0:T(8,128)(2,1)S(1)} %collective-permute-done.25), channel_id=1, source_target_pairs={{0,15},{1,0},{2,1},{3,2},{4,3},{5,4},{6,5},{7,6},{8,7},{9,8},{10,9... | collective-permute-start | bytes 202760 | tf_op jit(solution)/shard_map/ppermute | solution.py:20
  232.4 6.7 %collective-permute-start.27 = (bf16[24,1408]{1,0:T(8,128)(2,1)S(1)}, bf16[24,1408]{1,0:T(8,128)(2,1)}, u32[]{:S(2)}, u32[]{:S(2)}) collective-permute-start(bf16[24,1408]{1,0:T(8,128)(2,1)S(1)} %collective-permute-done.26), channel_id=1, source_target_pairs={{0,15},{1,0},{2,1},{3,2},{4,3},{5,4},{6,5},{7,6},{8,7},{9,8},{10,9... | collective-permute-start | bytes 202760 | tf_op jit(solution)/shard_map/ppermute | solution.py:20
  241.1 6.7 %collective-permute-start.28 = (bf16[24,1408]{1,0:T(8,128)(2,1)}, bf16[24,1408]{1,0:T(8,128)(2,1)}, u32[]{:S(2)}, u32[]{:S(2)}) collective-permute-start(bf16[24,1408]{1,0:T(8,128)(2,1)} %collective-permute-done.27), channel_id=1, source_target_pairs={{0,15},{1,0},{2,1},{3,2},{4,3},{5,4},{6,5},{7,6},{8,7},{9,8},{10,9... | collective-permute-start | bytes 202760 | tf_op jit(solution)/shard_map/ppermute | solution.py:20
  254.1 6.7 %collective-permute-start.29 = (bf16[24,1408]{1,0:T(8,128)(2,1)}, bf16[24,1408]{1,0:T(8,128)(2,1)S(1)}, u32[]{:S(2)}, u32[]{:S(2)}) collective-permute-start(bf16[24,1408]{1,0:T(8,128)(2,1)} %collective-permute-done.28), channel_id=1, source_target_pairs={{0,15},{1,0},{2,1},{3,2},{4,3},{5,4},{6,5},{7,6},{8,7},{9,8},{10,9... | collective-permute-start | bytes 202760 | tf_op jit(solution)/shard_map/ppermute | solution.py:20
  276.3 5.7 %convolution_convert_fusion = bf16[384,1408]{1,0:T(8,128)(2,1)} fusion(bf16[1408,384]{1,0:T(8,128)(2,1)} %reshape.123, bf16[1408,384]{1,0:T(8,128)(2,1)} %reshape.121, s32[]{:T(128)S(6)} %select_n.36, bf16[384,1408]{1,0:T(8,128)(2,1)} %constant_dynamic-update-slice_fusion.16), kind=kOutput, calls=%fused_computation | convolution fusion | flops 842760192 | bytes 4325380 | tf_op jit(solution)/shard_map/dot_general | solution.py:41
  282.7 90.9 %reduce-scatter.9.cloned.1.call-done = bf16[24,1408]{1,0:T(8,128)(2,1)} async-done(((bf16[384,1408]{1,0:T(8,128)(2,1)}), bf16[24,1408]{1,0:T(8,128)(2,1)}) %reduce-scatter.9.cloned.1.call-update) | async-done | bytes 67600
  379.2 6.2 %collective-permute-start.38 = (bf16[6,5632]{1,0:T(8,128)(2,1)S(1)}, bf16[6,5632]{1,0:T(8,128)(2,1)S(1)}, u32[]{:S(2)}, u32[]{:S(2)}) collective-permute-start(bf16[6,5632]{1,0:T(8,128)(2,1)S(1)} %reshape.117), channel_id=1, source_target_pairs={{0,15},{1,0},{2,1},{3,2},{4,3},{5,4},{6,5},{7,6},{8,7},{9,8},{10,9... | collective-permute-start | bytes 202760 | tf_op jit(solution)/shard_map/ppermute | solution.py:20
  387.3 6.7 %collective-permute-start.39 = (bf16[6,5632]{1,0:T(8,128)(2,1)S(1)}, bf16[6,5632]{1,0:T(8,128)(2,1)S(1)}, u32[]{:S(2)}, u32[]{:S(2)}) collective-permute-start(bf16[6,5632]{1,0:T(8,128)(2,1)S(1)} %collective-permute-done.38), channel_id=1, source_target_pairs={{0,15},{1,0},{2,1},{3,2},{4,3},{5,4},{6,5},{7,6},{8,7},{9,8},{10,9... | collective-permute-start | bytes 202760 | tf_op jit(solution)/shard_map/ppermute | solution.py:20
  396.0 6.7 %collective-permute-start.40 = (bf16[6,5632]{1,0:T(8,128)(2,1)S(1)}, bf16[6,5632]{1,0:T(8,128)(2,1)S(1)}, u32[]{:S(2)}, u32[]{:S(2)}) collective-permute-start(bf16[6,5632]{1,0:T(8,128)(2,1)S(1)} %collective-permute-done.39), channel_id=1, source_target_pairs={{0,15},{1,0},{2,1},{3,2},{4,3},{5,4},{6,5},{7,6},{8,7},{9,8},{10,9... | collective-permute-start | bytes 202760 | tf_op jit(solution)/shard_map/ppermute | solution.py:20
  405.3 6.7 %collective-permute-start.41 = (bf16[6,5632]{1,0:T(8,128)(2,1)S(1)}, bf16[6,5632]{1,0:T(8,128)(2,1)S(1)}, u32[]{:S(2)}, u32[]{:S(2)}) collective-permute-start(bf16[6,5632]{1,0:T(8,128)(2,1)S(1)} %collective-permute-done.40), channel_id=1, source_target_pairs={{0,15},{1,0},{2,1},{3,2},{4,3},{5,4},{6,5},{7,6},{8,7},{9,8},{10,9... | collective-permute-start | bytes 202760 | tf_op jit(solution)/shard_map/ppermute | solution.py:20
  415.5 6.7 %collective-permute-start.42 = (bf16[6,5632]{1,0:T(8,128)(2,1)S(1)}, bf16[6,5632]{1,0:T(8,128)(2,1)S(1)}, u32[]{:S(2)}, u32[]{:S(2)}) collective-permute-start(bf16[6,5632]{1,0:T(8,128)(2,1)S(1)} %collective-permute-done.41), channel_id=1, source_target_pairs={{0,15},{1,0},{2,1},{3,2},{4,3},{5,4},{6,5},{7,6},{8,7},{9,8},{10,9... | collective-permute-start | bytes 202760 | tf_op jit(solution)/shard_map/ppermute | solution.py:20
  424.3 6.7 %collective-permute-start.43 = (bf16[6,5632]{1,0:T(8,128)(2,1)S(1)}, bf16[6,5632]{1,0:T(8,128)(2,1)}, u32[]{:S(2)}, u32[]{:S(2)}) collective-permute-start(bf16[6,5632]{1,0:T(8,128)(2,1)S(1)} %collective-permute-done.42), channel_id=1, source_target_pairs={{0,15},{1,0},{2,1},{3,2},{4,3},{5,4},{6,5},{7,6},{8,7},{9,8},{10,9... | collective-permute-start | bytes 202760 | tf_op jit(solution)/shard_map/ppermute | solution.py:20
  433.1 6.7 %collective-permute-start.44 = (bf16[6,5632]{1,0:T(8,128)(2,1)}, bf16[6,5632]{1,0:T(8,128)(2,1)}, u32[]{:S(2)}, u32[]{:S(2)}) collective-permute-start(bf16[6,5632]{1,0:T(8,128)(2,1)} %collective-permute-done.43), channel_id=1, source_target_pairs={{0,15},{1,0},{2,1},{3,2},{4,3},{5,4},{6,5},{7,6},{8,7},{9,8},{10,9... | collective-permute-start | bytes 202760 | tf_op jit(solution)/shard_map/ppermute | solution.py:20
  442.0 6.8 %collective-permute-done.37 = bf16[6,5632]{1,0:T(8,128)(2,1)} collective-permute-done((bf16[6,5632]{1,0:T(8,128)(2,1)}, bf16[6,5632]{1,0:T(8,128)(2,1)}, u32[]{:S(2)}, u32[]{:S(2)}) %collective-permute-start.37) | collective-permute-done | bytes 67616 | tf_op jit(solution)/shard_map/ppermute | solution.py:18
  448.8 70.2 %concatenate.17 = bf16[192,5632]{1,0:T(8,128)(2,1)} concatenate(bf16[6,5632]{1,0:T(8,128)(2,1)} %collective-permute-done.37, bf16[6,5632]{1,0:T(8,128)(2,1)} %collective-permute-done.36, bf16[6,5632]{1,0:T(8,128)(2,1)} %copy-done.5, bf16[6,5632]{1,0:T(8,128)(2,1)} %copy-done.3, bf16[6,5632]{1,0:T(8,128)(2,1)} %collective-permute-done.33, ...), dimensions={0} | concatenate | bytes 4325376 | tf_op jit(solution)/shard_map/jit(_roll_dynamic)/concatenate | solution.py:22
  521.1 43.9 %all_to_all.5 = bf16[32,16,256]{2,1,0:T(8,128)(2,1)S(1)} all-to-all(bf16[32,16,256]{2,1,0:T(8,128)(2,1)S(1)} %bitcast.49), channel_id=1, replica_groups=mesh['tok'=32,'feat'=16] {'tok'}, dimensions={0} | all-to-all | bytes 524288 | tf_op jit(solution)/shard_map/all_to_all | solution.py:97
  (169 shorter events, 86.3 us)
Async XLA Ops:
  7.4 178.9 %reduce-scatter.7.cloned.1.call-start = ((), (), s32[]{:S(2)}) async-start(), calls=%async_computation.5 | async-start | bytes 1148928
  11.3 9.3 %collective-permute-start = (bf16[24,1408]{1,0:T(8,128)(2,1)S(1)}, bf16[24,1408]{1,0:T(8,128)(2,1)S(1)}, u32[]{:S(2)}, u32[]{:S(2)}) collective-permute-start(bf16[24,1408]{1,0:T(8,128)(2,1)S(1)} %fusion.70), channel_id=1, source_target_pairs={{0,1},{1,2},{2,3},{3,4},{4,5},{5,6},{6,7},{7,8},{8,9},{9,10},{10,1... | collective-permute-start | bytes 202760 | tf_op jit(solution)/shard_map/ppermute | solution.py:18
  37.9 8.8 %collective-permute-start.3 = (bf16[24,1408]{1,0:T(8,128)(2,1)S(1)}, bf16[24,1408]{1,0:T(8,128)(2,1)S(1)}, u32[]{:S(2)}, u32[]{:S(2)}) collective-permute-start(bf16[24,1408]{1,0:T(8,128)(2,1)S(1)} %collective-permute-done.2), channel_id=1, source_target_pairs={{0,1},{1,2},{2,3},{3,4},{4,5},{5,6},{6,7},{7,8},{8,9},{9,10},{10,1... | collective-permute-start | bytes 202760 | tf_op jit(solution)/shard_map/ppermute | solution.py:18
  39.8 8.8 %collective-permute-start.10 = (bf16[24,1408]{1,0:T(8,128)(2,1)S(1)}, bf16[24,1408]{1,0:T(8,128)(2,1)S(1)}, u32[]{:S(2)}, u32[]{:S(2)}) collective-permute-start(bf16[24,1408]{1,0:T(8,128)(2,1)S(1)} %collective-permute-done.9), channel_id=1, source_target_pairs={{0,15},{1,0},{2,1},{3,2},{4,3},{5,4},{6,5},{7,6},{8,7},{9,8},{10,9... | collective-permute-start | bytes 202760 | tf_op jit(solution)/shard_map/ppermute | solution.py:20
  46.7 9.2 %collective-permute-start.4 = (bf16[24,1408]{1,0:T(8,128)(2,1)S(1)}, bf16[24,1408]{1,0:T(8,128)(2,1)S(1)}, u32[]{:S(2)}, u32[]{:S(2)}) collective-permute-start(bf16[24,1408]{1,0:T(8,128)(2,1)S(1)} %collective-permute-done.3), channel_id=1, source_target_pairs={{0,1},{1,2},{2,3},{3,4},{4,5},{5,6},{6,7},{7,8},{8,9},{9,10},{10,1... | collective-permute-start | bytes 202760 | tf_op jit(solution)/shard_map/ppermute | solution.py:18
  48.6 9.2 %collective-permute-start.11 = (bf16[24,1408]{1,0:T(8,128)(2,1)S(1)}, bf16[24,1408]{1,0:T(8,128)(2,1)S(1)}, u32[]{:S(2)}, u32[]{:S(2)}) collective-permute-start(bf16[24,1408]{1,0:T(8,128)(2,1)S(1)} %collective-permute-done.10), channel_id=1, source_target_pairs={{0,15},{1,0},{2,1},{3,2},{4,3},{5,4},{6,5},{7,6},{8,7},{9,8},{10,9... | collective-permute-start | bytes 202760 | tf_op jit(solution)/shard_map/ppermute | solution.py:20
  55.9 8.6 %collective-permute-start.5 = (bf16[24,1408]{1,0:T(8,128)(2,1)S(1)}, bf16[24,1408]{1,0:T(8,128)(2,1)S(1)}, u32[]{:S(2)}, u32[]{:S(2)}) collective-permute-start(bf16[24,1408]{1,0:T(8,128)(2,1)S(1)} %collective-permute-done.4), channel_id=1, source_target_pairs={{0,1},{1,2},{2,3},{3,4},{4,5},{5,6},{6,7},{7,8},{8,9},{9,10},{10,1... | collective-permute-start | bytes 202760 | tf_op jit(solution)/shard_map/ppermute | solution.py:18
  57.8 8.6 %collective-permute-start.12 = (bf16[24,1408]{1,0:T(8,128)(2,1)S(1)}, bf16[24,1408]{1,0:T(8,128)(2,1)}, u32[]{:S(2)}, u32[]{:S(2)}) collective-permute-start(bf16[24,1408]{1,0:T(8,128)(2,1)S(1)} %collective-permute-done.11), channel_id=1, source_target_pairs={{0,15},{1,0},{2,1},{3,2},{4,3},{5,4},{6,5},{7,6},{8,7},{9,8},{10,9... | collective-permute-start | bytes 202760 | tf_op jit(solution)/shard_map/ppermute | solution.py:20
  64.6 8.7 %collective-permute-start.6 = (bf16[24,1408]{1,0:T(8,128)(2,1)S(1)}, bf16[24,1408]{1,0:T(8,128)(2,1)}, u32[]{:S(2)}, u32[]{:S(2)}) collective-permute-start(bf16[24,1408]{1,0:T(8,128)(2,1)S(1)} %collective-permute-done.5), channel_id=1, source_target_pairs={{0,1},{1,2},{2,3},{3,4},{4,5},{5,6},{6,7},{7,8},{8,9},{9,10},{10,1... | collective-permute-start | bytes 202760 | tf_op jit(solution)/shard_map/ppermute | solution.py:18
  66.5 8.7 %collective-permute-start.13 = (bf16[24,1408]{1,0:T(8,128)(2,1)}, bf16[24,1408]{1,0:T(8,128)(2,1)}, u32[]{:S(2)}, u32[]{:S(2)}) collective-permute-start(bf16[24,1408]{1,0:T(8,128)(2,1)} %collective-permute-done.12), channel_id=1, source_target_pairs={{0,15},{1,0},{2,1},{3,2},{4,3},{5,4},{6,5},{7,6},{8,7},{9,8},{10,9... | collective-permute-start | bytes 202760 | tf_op jit(solution)/shard_map/ppermute | solution.py:20
  73.2 8.8 %collective-permute-start.7 = (bf16[24,1408]{1,0:T(8,128)(2,1)}, bf16[24,1408]{1,0:T(8,128)(2,1)}, u32[]{:S(2)}, u32[]{:S(2)}) collective-permute-start(bf16[24,1408]{1,0:T(8,128)(2,1)} %collective-permute-done.6), channel_id=1, source_target_pairs={{0,1},{1,2},{2,3},{3,4},{4,5},{5,6},{6,7},{7,8},{8,9},{9,10},{10,1... | collective-permute-start | bytes 202760 | tf_op jit(solution)/shard_map/ppermute | solution.py:18
  75.2 12.4 %collective-permute-start.14 = (bf16[24,1408]{1,0:T(8,128)(2,1)}, bf16[24,1408]{1,0:T(8,128)(2,1)S(1)}, u32[]{:S(2)}, u32[]{:S(2)}) collective-permute-start(bf16[24,1408]{1,0:T(8,128)(2,1)} %collective-permute-done.13), channel_id=1, source_target_pairs={{0,15},{1,0},{2,1},{3,2},{4,3},{5,4},{6,5},{7,6},{8,7},{9,8},{10,9... | collective-permute-start | bytes 202760 | tf_op jit(solution)/shard_map/ppermute | solution.py:20
  92.5 157.3 %all-gather.5.cloned.1.call-start = ((), (), s32[]{:S(2)}) async-start(), calls=%async_computation.3 | async-start | bytes 1216512 | tf_op jit(solution)/shard_map/all_gather | solution.py:53
  93.0 158.9 %all-gather.7.cloned.1.call-start = ((), (), s32[]{:S(2)}) async-start(), calls=%async_computation.4 | async-start | bytes 1216512 | tf_op jit(solution)/shard_map/all_gather | solution.py:57
  93.6 280.0 %reduce-scatter.9.cloned.1.call-start = ((), (), s32[]{:S(2)}) async-start(), calls=%async_computation.6 | async-start | bytes 1148928
  223.8 8.6 %collective-permute-start.26 = (bf16[24,1408]{1,0:T(8,128)(2,1)S(1)}, bf16[24,1408]{1,0:T(8,128)(2,1)S(1)}, u32[]{:S(2)}, u32[]{:S(2)}) collective-permute-start(bf16[24,1408]{1,0:T(8,128)(2,1)S(1)} %collective-permute-done.25), channel_id=1, source_target_pairs={{0,15},{1,0},{2,1},{3,2},{4,3},{5,4},{6,5},{7,6},{8,7},{9,8},{10,9... | collective-permute-start | bytes 202760 | tf_op jit(solution)/shard_map/ppermute | solution.py:20
  230.5 8.6 %collective-permute-start.20 = (bf16[24,1408]{1,0:T(8,128)(2,1)S(1)}, bf16[24,1408]{1,0:T(8,128)(2,1)S(1)}, u32[]{:S(2)}, u32[]{:S(2)}) collective-permute-start(bf16[24,1408]{1,0:T(8,128)(2,1)S(1)} %collective-permute-done.19), channel_id=1, source_target_pairs={{0,1},{1,2},{2,3},{3,4},{4,5},{5,6},{6,7},{7,8},{8,9},{9,10},{10,1... | collective-permute-start | bytes 202760 | tf_op jit(solution)/shard_map/ppermute | solution.py:18
  232.4 8.6 %collective-permute-start.27 = (bf16[24,1408]{1,0:T(8,128)(2,1)S(1)}, bf16[24,1408]{1,0:T(8,128)(2,1)}, u32[]{:S(2)}, u32[]{:S(2)}) collective-permute-start(bf16[24,1408]{1,0:T(8,128)(2,1)S(1)} %collective-permute-done.26), channel_id=1, source_target_pairs={{0,15},{1,0},{2,1},{3,2},{4,3},{5,4},{6,5},{7,6},{8,7},{9,8},{10,9... | collective-permute-start | bytes 202760 | tf_op jit(solution)/shard_map/ppermute | solution.py:20
  239.2 8.7 %collective-permute-start.21 = (bf16[24,1408]{1,0:T(8,128)(2,1)S(1)}, bf16[24,1408]{1,0:T(8,128)(2,1)}, u32[]{:S(2)}, u32[]{:S(2)}) collective-permute-start(bf16[24,1408]{1,0:T(8,128)(2,1)S(1)} %collective-permute-done.20), channel_id=1, source_target_pairs={{0,1},{1,2},{2,3},{3,4},{4,5},{5,6},{6,7},{7,8},{8,9},{9,10},{10,1... | collective-permute-start | bytes 202760 | tf_op jit(solution)/shard_map/ppermute | solution.py:18
  241.1 13.0 %collective-permute-start.28 = (bf16[24,1408]{1,0:T(8,128)(2,1)}, bf16[24,1408]{1,0:T(8,128)(2,1)}, u32[]{:S(2)}, u32[]{:S(2)}) collective-permute-start(bf16[24,1408]{1,0:T(8,128)(2,1)} %collective-permute-done.27), channel_id=1, source_target_pairs={{0,15},{1,0},{2,1},{3,2},{4,3},{5,4},{6,5},{7,6},{8,7},{9,8},{10,9... | collective-permute-start | bytes 202760 | tf_op jit(solution)/shard_map/ppermute | solution.py:20
  247.8 13.0 %collective-permute-start.22 = (bf16[24,1408]{1,0:T(8,128)(2,1)}, bf16[24,1408]{1,0:T(8,128)(2,1)}, u32[]{:S(2)}, u32[]{:S(2)}) collective-permute-start(bf16[24,1408]{1,0:T(8,128)(2,1)} %collective-permute-done.21), channel_id=1, source_target_pairs={{0,1},{1,2},{2,3},{3,4},{4,5},{5,6},{6,7},{7,8},{8,9},{9,10},{10,1... | collective-permute-start | bytes 202760 | tf_op jit(solution)/shard_map/ppermute | solution.py:18
  254.1 21.5 %collective-permute-start.29 = (bf16[24,1408]{1,0:T(8,128)(2,1)}, bf16[24,1408]{1,0:T(8,128)(2,1)S(1)}, u32[]{:S(2)}, u32[]{:S(2)}) collective-permute-start(bf16[24,1408]{1,0:T(8,128)(2,1)} %collective-permute-done.28), channel_id=1, source_target_pairs={{0,15},{1,0},{2,1},{3,2},{4,3},{5,4},{6,5},{7,6},{8,7},{9,8},{10,9... | collective-permute-start | bytes 202760 | tf_op jit(solution)/shard_map/ppermute | solution.py:20
  396.0 9.4 %collective-permute-start.40 = (bf16[6,5632]{1,0:T(8,128)(2,1)S(1)}, bf16[6,5632]{1,0:T(8,128)(2,1)S(1)}, u32[]{:S(2)}, u32[]{:S(2)}) collective-permute-start(bf16[6,5632]{1,0:T(8,128)(2,1)S(1)} %collective-permute-done.39), channel_id=1, source_target_pairs={{0,15},{1,0},{2,1},{3,2},{4,3},{5,4},{6,5},{7,6},{8,7},{9,8},{10,9... | collective-permute-start | bytes 202760 | tf_op jit(solution)/shard_map/ppermute | solution.py:20
  402.7 9.3 %collective-permute-start.33 = (bf16[6,5632]{1,0:T(8,128)(2,1)S(1)}, bf16[6,5632]{1,0:T(8,128)(2,1)}, u32[]{:S(2)}, u32[]{:S(2)}) collective-permute-start(bf16[6,5632]{1,0:T(8,128)(2,1)S(1)} %collective-permute-done.32), channel_id=1, source_target_pairs={{0,1},{1,2},{2,3},{3,4},{4,5},{5,6},{6,7},{7,8},{8,9},{9,10},{10,1... | collective-permute-start | bytes 202760 | tf_op jit(solution)/shard_map/ppermute | solution.py:18
  405.3 9.5 %collective-permute-start.41 = (bf16[6,5632]{1,0:T(8,128)(2,1)S(1)}, bf16[6,5632]{1,0:T(8,128)(2,1)S(1)}, u32[]{:S(2)}, u32[]{:S(2)}) collective-permute-start(bf16[6,5632]{1,0:T(8,128)(2,1)S(1)} %collective-permute-done.40), channel_id=1, source_target_pairs={{0,15},{1,0},{2,1},{3,2},{4,3},{5,4},{6,5},{7,6},{8,7},{9,8},{10,9... | collective-permute-start | bytes 202760 | tf_op jit(solution)/shard_map/ppermute | solution.py:20
  412.0 10.2 %collective-permute-start.34 = (bf16[6,5632]{1,0:T(8,128)(2,1)}, bf16[6,5632]{1,0:T(8,128)(2,1)S(1)}, u32[]{:S(2)}, u32[]{:S(2)}) collective-permute-start(bf16[6,5632]{1,0:T(8,128)(2,1)} %collective-permute-done.33), channel_id=1, source_target_pairs={{0,1},{1,2},{2,3},{3,4},{4,5},{5,6},{6,7},{7,8},{8,9},{9,10},{10,1... | collective-permute-start | bytes 202760 | tf_op jit(solution)/shard_map/ppermute | solution.py:18
  415.5 8.8 %collective-permute-start.42 = (bf16[6,5632]{1,0:T(8,128)(2,1)S(1)}, bf16[6,5632]{1,0:T(8,128)(2,1)S(1)}, u32[]{:S(2)}, u32[]{:S(2)}) collective-permute-start(bf16[6,5632]{1,0:T(8,128)(2,1)S(1)} %collective-permute-done.41), channel_id=1, source_target_pairs={{0,15},{1,0},{2,1},{3,2},{4,3},{5,4},{6,5},{7,6},{8,7},{9,8},{10,9... | collective-permute-start | bytes 202760 | tf_op jit(solution)/shard_map/ppermute | solution.py:20
  422.2 8.8 %collective-permute-start.35 = (bf16[6,5632]{1,0:T(8,128)(2,1)S(1)}, bf16[6,5632]{1,0:T(8,128)(2,1)S(1)}, u32[]{:S(2)}, u32[]{:S(2)}) collective-permute-start(bf16[6,5632]{1,0:T(8,128)(2,1)S(1)} %collective-permute-done.34), channel_id=1, source_target_pairs={{0,1},{1,2},{2,3},{3,4},{4,5},{5,6},{6,7},{7,8},{8,9},{9,10},{10,1... | collective-permute-start | bytes 202760 | tf_op jit(solution)/shard_map/ppermute | solution.py:18
  424.3 8.8 %collective-permute-start.43 = (bf16[6,5632]{1,0:T(8,128)(2,1)S(1)}, bf16[6,5632]{1,0:T(8,128)(2,1)}, u32[]{:S(2)}, u32[]{:S(2)}) collective-permute-start(bf16[6,5632]{1,0:T(8,128)(2,1)S(1)} %collective-permute-done.42), channel_id=1, source_target_pairs={{0,15},{1,0},{2,1},{3,2},{4,3},{5,4},{6,5},{7,6},{8,7},{9,8},{10,9... | collective-permute-start | bytes 202760 | tf_op jit(solution)/shard_map/ppermute | solution.py:20
  431.1 8.7 %collective-permute-start.36 = (bf16[6,5632]{1,0:T(8,128)(2,1)S(1)}, bf16[6,5632]{1,0:T(8,128)(2,1)}, u32[]{:S(2)}, u32[]{:S(2)}) collective-permute-start(bf16[6,5632]{1,0:T(8,128)(2,1)S(1)} %collective-permute-done.35), channel_id=1, source_target_pairs={{0,1},{1,2},{2,3},{3,4},{4,5},{5,6},{6,7},{7,8},{8,9},{9,10},{10,1... | collective-permute-start | bytes 202760 | tf_op jit(solution)/shard_map/ppermute | solution.py:18
  433.1 8.8 %collective-permute-start.44 = (bf16[6,5632]{1,0:T(8,128)(2,1)}, bf16[6,5632]{1,0:T(8,128)(2,1)}, u32[]{:S(2)}, u32[]{:S(2)}) collective-permute-start(bf16[6,5632]{1,0:T(8,128)(2,1)} %collective-permute-done.43), channel_id=1, source_target_pairs={{0,15},{1,0},{2,1},{3,2},{4,3},{5,4},{6,5},{7,6},{8,7},{9,8},{10,9... | collective-permute-start | bytes 202760 | tf_op jit(solution)/shard_map/ppermute | solution.py:20
  439.8 8.9 %collective-permute-start.37 = (bf16[6,5632]{1,0:T(8,128)(2,1)}, bf16[6,5632]{1,0:T(8,128)(2,1)}, u32[]{:S(2)}, u32[]{:S(2)}) collective-permute-start(bf16[6,5632]{1,0:T(8,128)(2,1)} %collective-permute-done.36), channel_id=1, source_target_pairs={{0,1},{1,2},{2,3},{3,4},{4,5},{5,6},{6,7},{7,8},{8,9},{9,10},{10,1... | collective-permute-start | bytes 202760 | tf_op jit(solution)/shard_map/ppermute | solution.py:18
  (33 other events, 953.3 us)
Sparse Core Ops, SparseCore 0:
  92.6 93.6 reduce-scatter.6
  282.1 91.4 reduce-scatter.8
Sparse Core Ops, SparseCore 1:
  95.0 78.9 all-gather.4
  176.0 68.3 all-gather.6
